TPU v7x, 128 devices: a whole 4x4x4 slice. The times are simulated.
128 devices in a mesh: leaf: 8 (over x, core), blk: 16 (over z, y).
Axes of the slice: x: 4, y: 4, z: 4, core: 2. Of those that a mesh axis runs over, the one named last changes fastest.
Arguments:
- right_side: float32 [4, 8, 16, 512], P(None, 'leaf', 'blk'), may hold values from -6 to 6
- diag_inverse: bfloat16 [8, 16, 128, 30720], P('leaf', 'blk'), as said below
- update_factor: bfloat16 [8, 16, 128, 69632], P('leaf', 'blk'), may hold values from -0.046875 to 0.046875
- live_blocks: int32 [15], replicated, may hold values from 1 to 128, as said below
Outputs:
- forward_solution: float32 [4, 8, 16, 512], P(None, 'leaf', 'blk')
- solution: float32 [4, 8, 16, 512], P(None, 'leaf', 'blk')
Inputs may be any that keep to these rules, and one draw needn't show every extreme that they name: `live_blocks`: A supernode with 2^l * 16 block-rows (level l, listed level by level from level 0, by group within a level) has between a quarter of them (at least 1) and all of them live; the root supernode (the last entry) has all of them live. `diag_inverse`: each level's inverse diagonal block is lower triangular in its supernode's row order, with a positive diagonal.
All inputs are finite; a program needn't handle non-finite values.
Results may differ from a plain program's by a relative error of at most 0.009.
Values sent between devices are 32-bit elements; how exact they have to be, the bound alone decides.
A program may use at most 128 MiB of HBM per device.

v0:
```python
import jax
import jax.numpy as jnp
from jax import lax
from jax.sharding import Mesh
from jax.sharding import PartitionSpec as P

BLK = ("blk_0", "blk_1")
LEAF = ("leaf_0", "leaf_1")


def padded_to(lines, count):
    spare = -lines.shape[0] % count
    if not spare:
        return lines
    return jnp.concatenate([lines, jnp.zeros((spare, *lines.shape[1:]), lines.dtype)])


def sent_to_all(array, axis):
    count = lax.axis_size(axis)
    return lax.all_to_all(
        jnp.broadcast_to(array[None], (count, *array.shape)), axis, 0, 0, tiled=True
    )


def in_order(parts, dim):
    lengths = list(parts.shape[1:])
    lengths[dim] *= parts.shape[0]
    return jnp.moveaxis(parts, 0, dim).reshape(lengths)


def gathered_copies(array, axis, dim):
    parts = sent_to_all(array, axis)
    return in_order(parts, dim)


def cut_along(array, dim, count):
    lengths = array.shape
    parts = array.reshape(*lengths[:dim], count, lengths[dim] // count, *lengths[dim + 1 :])
    return jnp.moveaxis(parts, dim, 0)


def sent_and_summed(array, axis, dim):
    count = lax.axis_size(axis)
    parts = lax.all_to_all(cut_along(array, dim, count), axis, 0, 0, tiled=True)
    return jnp.sum(parts, axis=0)


def nested_sum(array, axes):
    lines = array.reshape(-1)
    padded = padded_to(lines, lax.axis_size(axes))
    whole = gathered_copies(sent_and_summed(padded, axes, 0), axes, 0)
    return lax.slice_in_dim(whole, 0, len(lines)).reshape(array.shape)


def swapped(block, axis, apart):
    count = lax.axis_size(axis)
    route = []
    for low in range(count):
        high = low | 1 << apart
        if high != low and high < count:
            route += [(low, high), (high, low)]
    return lax.ppermute(block, axis, route)


def gather_axes(array, axes, dim):
    far, near = axes
    leading = sent_to_all(array, far)
    parts = jnp.swapaxes(sent_to_all(leading, near), 0, 1)
    return in_order(parts.reshape(-1, *array.shape), dim)


def group_sum(partial_value, height):
    current = nested_sum(partial_value, BLK)
    for bit_number in range(height):
        current = current + swapped(current, LEAF, bit_number)
    return current


def local(right_side, diag_inverse, update_factor, live_blocks):
    leaf_count = lax.axis_size(LEAF)
    block_count = lax.axis_size(BLK)
    levels = leaf_count.bit_length()
    leaf_index = lax.axis_index(LEAF)
    block_index = lax.axis_index(BLK)
    block_rows = diag_inverse.shape[2]
    vectors = right_side.shape[0]
    level_width = block_count * block_rows
    rows_all = leaf_count * level_width
    flat_side = right_side.reshape(vectors, 1, levels * block_rows)
    every_side = gather_axes(flat_side, (("leaf_0", "leaf_1", "blk_0"), "blk_1"), 1)
    inverse_rows = diag_inverse.reshape(block_rows, -1)
    update_rows = update_factor.reshape(block_rows, -1)
    orders = [(1 << height) * level_width for height in range(levels)]
    spans = [sum(orders[height + 1 :]) for height in range(levels)]
    update_start = [sum(spans[:height]) for height in range(levels)]
    contract_second = (((1,), (1,)), ((), ()))
    own_masks = []
    group_masks = []
    own_starts = []
    group_starts = []
    inverse_parts = []
    update_parts = []
    for height in range(levels):
        group_index = leaf_index >> height
        local_rank = leaf_index & (1 << height) - 1
        offset = 2 * leaf_count - (2 * leaf_count >> height)
        live_count = live_blocks[offset + group_index]
        own_position = local_rank * block_count + block_index
        own_masks.append((own_position < live_count).astype(jnp.float32))
        block_alive = (jnp.arange((1 << height) * block_count) < live_count).astype(jnp.float32)
        group_masks.append(jnp.repeat(block_alive, block_rows))
        own_starts.append(own_position * block_rows)
        group_starts.append(group_index * orders[height])
        start = ((1 << height) - 1) * level_width
        inverse_parts.append(inverse_rows[:, start : start + orders[height]])
        update_parts.append(
            update_rows[:, update_start[height] : update_start[height] + spans[height]]
        )
    pending = [jnp.zeros((vectors, orders[height]), jnp.float32) for height in range(levels)]
    forward = []
    for height in range(levels):
        level_side = every_side[:, :, height * block_rows : (height + 1) * block_rows].reshape(
            vectors, rows_all
        )
        source = lax.dynamic_slice_in_dim(level_side, group_starts[height], orders[height], 1)
        if height > 0:
            source = source - group_sum(pending[height], height)
        reduced = (group_masks[height] * source).astype(jnp.bfloat16)
        solved = own_masks[height] * lax.dot_general(
            reduced, inverse_parts[height], contract_second, preferred_element_type=jnp.float32
        )
        forward.append(solved)
        if height < levels - 1:
            spread = jnp.dot(
                solved.astype(jnp.bfloat16),
                update_parts[height],
                preferred_element_type=jnp.float32,
            )
            cursor = 0
            for ancestor in range(height + 1, levels):
                pending[ancestor] = (
                    pending[ancestor] + spread[:, cursor : cursor + orders[ancestor]]
                )
                cursor += orders[ancestor]
    whole_solved = [None] * levels
    backward = [None] * levels
    for height in reversed(range(levels)):
        residual = forward[height]
        if height < levels - 1:
            ancestors = jnp.concatenate(
                [whole_solved[ancestor] for ancestor in range(height + 1, levels)], axis=1
            )
            residual = residual - lax.dot_general(
                ancestors, update_parts[height], contract_second, preferred_element_type=jnp.float32
            )
        weighted = (own_masks[height] * residual).astype(jnp.bfloat16)
        partial_value = jnp.dot(weighted, inverse_parts[height], preferred_element_type=jnp.float32)
        supernode_solved = group_masks[height] * group_sum(partial_value, height)
        backward[height] = lax.dynamic_slice_in_dim(
            supernode_solved, own_starts[height], block_rows, 1
        )
        whole_solved[height] = supernode_solved.astype(jnp.bfloat16)
    forward_out = jnp.stack(forward, axis=1).reshape(vectors, 1, 1, levels * block_rows)
    backward_out = jnp.stack(backward, axis=1).reshape(vectors, 1, 1, levels * block_rows)
    return (forward_out, backward_out)


def solution(mesh):
    split = Mesh(mesh.devices.reshape(4, 2, 4, 4), ("leaf_0", "leaf_1", "blk_0", "blk_1"))
    return jax.shard_map(
        local,
        mesh=split,
        in_specs=(
            P(None, LEAF, BLK, None),
            P(LEAF, BLK, None, None),
            P(LEAF, BLK, None, None),
            P(),
        ),
        out_specs=(P(None, LEAF, BLK, None), P(None, LEAF, BLK, None)),
        check_vma=False,
    )
```

profile of v0, /device:TPU:0, one launch (start us, length us, event | category | flops | bytes accessed | tf_op | source)
XLA Modules:
  0.0 300.4 jit_solution(17229657441119680006)
XLA Ops:
  1.4 17.2 %all_to_all.122 = f32[32,4,1,512]{3,1,2,0:T(4,128)S(1)} all-to-all(f32[32,4,1,512]{3,1,2,0:T(4,128)S(1)} %broadcast_in_dim.32), channel_id=1, replica_groups=mesh['leaf_0'=4,'leaf_1'=2,'blk_0'=4,'blk_1'=4] {'leaf_0','leaf_1','blk_0'}, dimensions={0} | all-to-all | bytes 524288 | tf_op jit(solution)/shard_map/all_to_all | solution.py:20
  26.9 12.5 %all-to-all-done.1 = f32[4,32,4,1,512]{4,1,2,3,0:T(8,128)S(1)} async-done(((f32[4,32,4,1,512]{4,1,2,3,0:T(8,128)}), f32[4,32,4,1,512]{4,1,2,3,0:T(8,128)S(1)}, u32[]{:S(2)}, u32[]{:S(2)}) %all-to-all-start.1) | async-done | bytes 1048608 | tf_op jit(solution)/shard_map/all_to_all | solution.py:20
  45.8 10.6 %all_to_all.123 = f32[16,1,1024]{2,1,0:T(1,128)S(1)} all-to-all(f32[16,1,1024]{2,1,0:T(1,128)S(1)} %all_to_all.99), channel_id=1, replica_groups=mesh['leaf_0'=4,'leaf_1'=2,'blk_0'=4,'blk_1'=4] {'blk_0','blk_1'}, dimensions={0} | all-to-all | bytes 131072 | tf_op jit(solution)/shard_map/all_to_all | solution.py:44
  61.3 6.9 %all-to-all-done.3 = f32[16,1,1024]{2,1,0:T(1,128)S(1)} async-done(((f32[16,1,1024]{2,1,0:T(1,128)}), f32[16,1,1024]{2,1,0:T(1,128)S(1)}, u32[]{:S(2)}, u32[]{:S(2)}) %all-to-all-start.3) | async-done | bytes 65568 | tf_op jit(solution)/shard_map/all_to_all | solution.py:20
  75.3 11.2 %all_to_all.124 = f32[16,1,2048]{2,1,0:T(1,128)S(1)} all-to-all(f32[16,1,2048]{2,1,0:T(1,128)S(1)} %all_to_all.100), channel_id=1, replica_groups=mesh['leaf_0'=4,'leaf_1'=2,'blk_0'=4,'blk_1'=4] {'blk_0','blk_1'}, dimensions={0} | all-to-all | bytes 262144 | tf_op jit(solution)/shard_map/all_to_all | solution.py:44
  86.6 11.1 %all_to_all.125 = f32[16,1,2048]{2,1,0:T(1,128)S(1)} all-to-all(f32[16,1,2048]{2,1,0:T(1,128)S(1)} %broadcast_in_dim.38), channel_id=1, replica_groups=mesh['leaf_0'=4,'leaf_1'=2,'blk_0'=4,'blk_1'=4] {'blk_0','blk_1'}, dimensions={0} | all-to-all | bytes 262144 | tf_op jit(solution)/shard_map/all_to_all | solution.py:20
  100.4 5.2 %collective-permute-done.2 = f32[4,8192]{1,0:T(4,128)S(1)} collective-permute-done((f32[4,8192]{1,0:T(4,128)S(1)}, f32[4,8192]{1,0:T(4,128)S(1)}, u32[]{:S(2)}, u32[]{:S(2)}) %collective-permute-start.2) | collective-permute-done | bytes 131104 | tf_op jit(solution)/shard_map/ppermute | solution.py:62
  111.1 11.8 %all_to_all.126 = f32[16,1,4096]{2,1,0:T(1,128)S(1)} all-to-all(f32[16,1,4096]{2,1,0:T(1,128)S(1)} %all_to_all.101), channel_id=1, replica_groups=mesh['leaf_0'=4,'leaf_1'=2,'blk_0'=4,'blk_1'=4] {'blk_0','blk_1'}, dimensions={0} | all-to-all | bytes 524288 | tf_op jit(solution)/shard_map/all_to_all | solution.py:44
  123.2 11.6 %all_to_all.127 = f32[16,1,4096]{2,1,0:T(1,128)S(1)} all-to-all(f32[16,1,4096]{2,1,0:T(1,128)S(1)} %broadcast_in_dim.79), channel_id=1, replica_groups=mesh['leaf_0'=4,'leaf_1'=2,'blk_0'=4,'blk_1'=4] {'blk_0','blk_1'}, dimensions={0} | all-to-all | bytes 524288 | tf_op jit(solution)/shard_map/all_to_all | solution.py:20
  139.3 6.4 %collective-permute-done.4 = f32[4,16384]{1,0:T(4,128)S(1)} collective-permute-done((f32[4,16384]{1,0:T(4,128)S(1)}, f32[4,16384]{1,0:T(4,128)S(1)}, u32[]{:S(2)}, u32[]{:S(2)}) %collective-permute-start.4) | collective-permute-done | bytes 262176 | tf_op jit(solution)/shard_map/ppermute | solution.py:62
  147.2 7.9 %collective-permute-done.5 = f32[4,16384]{1,0:T(4,128)S(1)} collective-permute-done((f32[4,16384]{1,0:T(4,128)S(1)}, f32[4,16384]{1,0:T(4,128)S(1)}, u32[]{:S(2)}, u32[]{:S(2)}) %collective-permute-start.5) | collective-permute-done | bytes 262176 | tf_op jit(solution)/shard_map/ppermute | solution.py:62
  161.7 11.6 %all_to_all.128 = f32[16,1,4096]{2,1,0:T(1,128)S(1)} all-to-all(f32[16,1,4096]{2,1,0:T(1,128)S(1)} %all_to_all.102), channel_id=1, replica_groups=mesh['leaf_0'=4,'leaf_1'=2,'blk_0'=4,'blk_1'=4] {'blk_0','blk_1'}, dimensions={0} | all-to-all | bytes 524288 | tf_op jit(solution)/shard_map/all_to_all | solution.py:44
  173.6 11.6 %all_to_all.129 = f32[16,1,4096]{2,1,0:T(1,128)S(1)} all-to-all(f32[16,1,4096]{2,1,0:T(1,128)S(1)} %broadcast_in_dim.80), channel_id=1, replica_groups=mesh['leaf_0'=4,'leaf_1'=2,'blk_0'=4,'blk_1'=4] {'blk_0','blk_1'}, dimensions={0} | all-to-all | bytes 524288 | tf_op jit(solution)/shard_map/all_to_all | solution.py:20
  188.4 7.7 %collective-permute-done.7 = f32[4,16384]{1,0:T(4,128)S(1)} collective-permute-done((f32[4,16384]{1,0:T(4,128)S(1)}, f32[4,16384]{1,0:T(4,128)S(1)}, u32[]{:S(2)}, u32[]{:S(2)}) %collective-permute-start.7) | collective-permute-done | bytes 262176 | tf_op jit(solution)/shard_map/ppermute | solution.py:62
  197.4 8.0 %collective-permute-done.8 = f32[4,16384]{1,0:T(4,128)S(1)} collective-permute-done((f32[4,16384]{1,0:T(4,128)S(1)}, f32[4,16384]{1,0:T(4,128)S(1)}, u32[]{:S(2)}, u32[]{:S(2)}) %collective-permute-start.8) | collective-permute-done | bytes 262176 | tf_op jit(solution)/shard_map/ppermute | solution.py:62
  205.4 5.0 %fusion.15 = f32[4,8192]{1,0:T(4,128)S(1)} fusion(bf16[128,30720]{1,0:T(8,128)(2,1)} %bitcast.62, f32[4,128]{1,0:T(4,128)S(1)} %fusion.19, bf16[4,16384]{1,0:T(4,128)(2,1)S(1)} %get-tuple-element.12, bf16[128,69632]{1,0:T(8,128)(2,1)} %bitcast.54, f32[]{:T(128)S(6)} %convert_element_type.73), kind=kOutput, calls=%fused_computation.16 | convolution fusion | flops 25167360 | bytes 6555652 | tf_op jit(solution)/shard_map/dot_general | solution.py:157
  210.6 10.9 %all_to_all.130 = f32[16,1,2048]{2,1,0:T(1,128)S(1)} all-to-all(f32[16,1,2048]{2,1,0:T(1,128)S(1)} %all_to_all.103), channel_id=1, replica_groups=mesh['leaf_0'=4,'leaf_1'=2,'blk_0'=4,'blk_1'=4] {'blk_0','blk_1'}, dimensions={0} | all-to-all | bytes 262144 | tf_op jit(solution)/shard_map/all_to_all | solution.py:44
  221.7 11.1 %all_to_all.131 = f32[16,1,2048]{2,1,0:T(1,128)S(1)} all-to-all(f32[16,1,2048]{2,1,0:T(1,128)S(1)} %broadcast_in_dim.81), channel_id=1, replica_groups=mesh['leaf_0'=4,'leaf_1'=2,'blk_0'=4,'blk_1'=4] {'blk_0','blk_1'}, dimensions={0} | all-to-all | bytes 262144 | tf_op jit(solution)/shard_map/all_to_all | solution.py:20
  240.3 5.3 %fusion.50 = f32[4,4096]{1,0:T(4,128)S(1)} fusion(f32[4,128]{1,0:T(4,128)S(1)} %convolution_multiply_fusion, bf16[128,69632]{1,0:T(8,128)(2,1)} %bitcast.55, bf16[128,30720]{1,0:T(8,128)(2,1)} %bitcast.63, bf16[4,16384]{1,0:T(4,128)(2,1)S(1)} %get-tuple-element.12, bf16[4,8192]{1,0:T(4,128)(2,1)S(1)} %get-tuple-element.10, f32[]{:T(128)S(6)} %convert_element_type.69), kind=kOutput, calls=%fused_computation.32 | convolution fusion | flops 29754880 | bytes 7604228 | tf_op jit(solution)/shard_map/dot_general | solution.py:157
  249.9 7.5 %all-to-all-done.12 = f32[16,1,1024]{2,1,0:T(1,128)S(1)} async-done(((f32[16,1,1024]{2,1,0:T(1,128)}), f32[16,1,1024]{2,1,0:T(1,128)S(1)}, u32[]{:S(2)}, u32[]{:S(2)}) %all-to-all-start.12) | async-done | bytes 65568 | tf_op jit(solution)/shard_map/all_to_all | solution.py:44
  262.2 7.0 %all-to-all-done.13 = f32[16,1,1024]{2,1,0:T(1,128)S(1)} async-done(((f32[16,1,1024]{2,1,0:T(1,128)}), f32[16,1,1024]{2,1,0:T(1,128)S(1)}, u32[]{:S(2)}, u32[]{:S(2)}) %all-to-all-start.13) | async-done | bytes 65568 | tf_op jit(solution)/shard_map/all_to_all | solution.py:20
  270.8 5.4 %fusion.56 = f32[4,2048]{1,0:T(4,128)S(1)} fusion(f32[4,128]{1,0:T(4,128)S(1)} %convolution_multiply_fusion.1, bf16[128,69632]{1,0:T(8,128)(2,1)} %bitcast.56, bf16[128,30720]{1,0:T(8,128)(2,1)} %bitcast.64, bf16[4,16384]{1,0:T(4,128)(2,1)S(1)} %get-tuple-element.12, bf16[4,8192]{1,0:T(4,128)(2,1)S(1)} %get-tuple-element.10, ...), kind=kOutput, calls=%fused_computation.34 | convolution fusion | flops 32146944 | bytes 8128516 | tf_op jit(solution)/shard_map/dot_general | solution.py:157
  280.4 7.5 %all-to-all-done.14 = f32[16,1,512]{2,1,0:T(1,128)S(1)} async-done(((f32[16,1,512]{2,1,0:T(1,128)}), f32[16,1,512]{2,1,0:T(1,128)S(1)}, u32[]{:S(2)}, u32[]{:S(2)}) %all-to-all-start.14) | async-done | bytes 32800 | tf_op jit(solution)/shard_map/all_to_all | solution.py:44
  292.1 7.5 %all-to-all-done.15 = f32[16,1,512]{2,1,0:T(1,128)S(1)} async-done(((f32[16,1,512]{2,1,0:T(1,128)}), f32[16,1,512]{2,1,0:T(1,128)S(1)}, u32[]{:S(2)}, u32[]{:S(2)}) %all-to-all-start.15) | async-done | bytes 32800 | tf_op jit(solution)/shard_map/all_to_all | solution.py:20
  (102 shorter events, 78.4 us)
Async XLA Ops:
  19.8 19.7 %all-to-all-start.1 = ((f32[4,32,4,1,512]{4,1,2,3,0:T(8,128)}), f32[4,32,4,1,512]{4,1,2,3,0:T(8,128)S(1)}, u32[]{:S(2)}, u32[]{:S(2)}) async-start(f32[4,32,4,1,512]{4,1,2,3,0:T(8,128)} %broadcast_in_dim.34), calls=%async_computation.1 | async-start | bytes 2097152 | tf_op jit(solution)/shard_map/all_to_all | solution.py:20
  57.1 11.1 %all-to-all-start.3 = ((f32[16,1,1024]{2,1,0:T(1,128)}), f32[16,1,1024]{2,1,0:T(1,128)S(1)}, u32[]{:S(2)}, u32[]{:S(2)}) async-start(f32[16,1,1024]{2,1,0:T(1,128)} %broadcast_in_dim.36), calls=%async_computation.3 | async-start | bytes 131072 | tf_op jit(solution)/shard_map/all_to_all | solution.py:20
  68.4 1.3 collective-permute-start
  98.1 1.5 collective-permute-start.1
  99.6 6.0 %collective-permute-start.2 = (f32[4,8192]{1,0:T(4,128)S(1)}, f32[4,8192]{1,0:T(4,128)S(1)}, u32[]{:S(2)}, u32[]{:S(2)}) collective-permute-start(f32[4,8192]{1,0:T(4,128)S(1)} %add.112), channel_id=1, source_target_pairs={{0,32},{32,0},{16,48},{48,16},{64,96},{96,64},{80,112},{112,80},{1... | collective-permute-start | bytes 393224 | tf_op jit(solution)/shard_map/ppermute | solution.py:62
  135.6 1.6 collective-permute-start.3
  137.3 8.4 %collective-permute-start.4 = (f32[4,16384]{1,0:T(4,128)S(1)}, f32[4,16384]{1,0:T(4,128)S(1)}, u32[]{:S(2)}, u32[]{:S(2)}) collective-permute-start(f32[4,16384]{1,0:T(4,128)S(1)} %add.118), channel_id=1, source_target_pairs={{0,32},{32,0},{16,48},{48,16},{64,96},{96,64},{80,112},{112,80},{1... | collective-permute-start | bytes 786440 | tf_op jit(solution)/shard_map/ppermute | solution.py:62
  145.8 9.3 %collective-permute-start.5 = (f32[4,16384]{1,0:T(4,128)S(1)}, f32[4,16384]{1,0:T(4,128)S(1)}, u32[]{:S(2)}, u32[]{:S(2)}) collective-permute-start(f32[4,16384]{1,0:T(4,128)S(1)} %add.119), channel_id=1, source_target_pairs={{0,64},{64,0},{16,80},{80,16},{32,96},{96,32},{48,112},{112,48},{1... | collective-permute-start | bytes 786440 | tf_op jit(solution)/shard_map/ppermute | solution.py:62
  186.0 1.6 collective-permute-start.6
  187.7 8.4 %collective-permute-start.7 = (f32[4,16384]{1,0:T(4,128)S(1)}, f32[4,16384]{1,0:T(4,128)S(1)}, u32[]{:S(2)}, u32[]{:S(2)}) collective-permute-start(f32[4,16384]{1,0:T(4,128)S(1)} %add.121), channel_id=1, source_target_pairs={{0,32},{32,0},{16,48},{48,16},{64,96},{96,64},{80,112},{112,80},{1... | collective-permute-start | bytes 786440 | tf_op jit(solution)/shard_map/ppermute | solution.py:62
  196.2 9.1 %collective-permute-start.8 = (f32[4,16384]{1,0:T(4,128)S(1)}, f32[4,16384]{1,0:T(4,128)S(1)}, u32[]{:S(2)}, u32[]{:S(2)}) collective-permute-start(f32[4,16384]{1,0:T(4,128)S(1)} %add.122), channel_id=1, source_target_pairs={{0,64},{64,0},{16,80},{80,16},{32,96},{96,32},{48,112},{112,48},{1... | collective-permute-start | bytes 786440 | tf_op jit(solution)/shard_map/ppermute | solution.py:62
  233.1 1.4 collective-permute-start.9
  234.6 5.6 %collective-permute-start.10 = (f32[4,8192]{1,0:T(4,128)S(1)}, f32[4,8192]{1,0:T(4,128)S(1)}, u32[]{:S(2)}, u32[]{:S(2)}) collective-permute-start(f32[4,8192]{1,0:T(4,128)S(1)} %add.124), channel_id=1, source_target_pairs={{0,32},{32,0},{16,48},{48,16},{64,96},{96,64},{80,112},{112,80},{1... | collective-permute-start | bytes 393224 | tf_op jit(solution)/shard_map/ppermute | solution.py:62
  246.3 11.1 %all-to-all-start.12 = ((f32[16,1,1024]{2,1,0:T(1,128)}), f32[16,1,1024]{2,1,0:T(1,128)S(1)}, u32[]{:S(2)}, u32[]{:S(2)}) async-start(f32[16,1,1024]{2,1,0:T(1,128)} %all_to_all.104), calls=%async_computation.12 | async-start | bytes 131072 | tf_op jit(solution)/shard_map/all_to_all | solution.py:44
  258.1 11.1 %all-to-all-start.13 = ((f32[16,1,1024]{2,1,0:T(1,128)}), f32[16,1,1024]{2,1,0:T(1,128)S(1)}, u32[]{:S(2)}, u32[]{:S(2)}) async-start(f32[16,1,1024]{2,1,0:T(1,128)} %broadcast_in_dim.82), calls=%async_computation.13 | async-start | bytes 131072 | tf_op jit(solution)/shard_map/all_to_all | solution.py:20
  269.4 1.3 collective-permute-start.11
  276.9 11.0 %all-to-all-start.14 = ((f32[16,1,512]{2,1,0:T(1,128)}), f32[16,1,512]{2,1,0:T(1,128)S(1)}, u32[]{:S(2)}, u32[]{:S(2)}) async-start(f32[16,1,512]{2,1,0:T(1,128)} %all_to_all.105), calls=%async_computation.14 | async-start | bytes 65536 | tf_op jit(solution)/shard_map/all_to_all | solution.py:44
  288.6 11.0 %all-to-all-start.15 = ((f32[16,1,512]{2,1,0:T(1,128)}), f32[16,1,512]{2,1,0:T(1,128)S(1)}, u32[]{:S(2)}, u32[]{:S(2)}) async-start(f32[16,1,512]{2,1,0:T(1,128)} %broadcast_in_dim.83), calls=%async_computation.15 | async-start | bytes 65536 | tf_op jit(solution)/shard_map/all_to_all | solution.py:20
where the time goes:
time: 302 us; the launch traced here: 300 us
  blocking collectives  118 us (39%)
  waiting for transfers between devices  95.2 us (32%)
  matrix products  37.7 us (12%)
  starting transfers between devices  27.7 us (9%)
  local copies, waits for them, and re-layouts  10.9 us (4%)
  other arithmetic  6.69 us (2%)
  between operations  3.61 us (1%)
    all_to_all x5, blocking collectives, sent_to_all(): lax.all_to_all(jnp.broadcast_to(array[None], (count, *array.shape)), axis...  62.5 us
    all_to_all x5, blocking collectives, sent_and_summed(): parts = lax.all_to_all(cut_along(array, dim, count), axis, 0, 0, tiled=True)  56 us
    ppermute x12, waiting for transfers between devices, swapped(): return lax.ppermute(block, axis, route)  46.2 us
    all_to_all x4, waiting for transfers between devices, sent_to_all(): lax.all_to_all(jnp.broadcast_to(array[None], (count, *array.shape)), axis...  34 us
    dot_general x4, matrix products, local(): jnp.dot(weighted, inverse_parts[height], preferred_element_type=jnp.float32)  18.5 us
    all_to_all x2, waiting for transfers between devices, sent_and_summed(): parts = lax.all_to_all(cut_along(array, dim, count), axis, 0, 0, tiled=True)  15 us
    all_to_all x4, starting transfers between devices, sent_to_all(): lax.all_to_all(jnp.broadcast_to(array[None], (count, *array.shape)), axis...  14.9 us
    dot_general x3, matrix products, local(): jnp.dot(solved.astype(jnp.bfloat16), update_parts[height], preferred_elem...  10.7 us
  transfers between devices with their start and end apart: 18, of which 17 were waited for; matrix products, arithmetic and copies ran while one was open for 2% of the time, Pallas kernels for 0%

commit v1 on v0

v1 whole, which is shorter than its diff:
```python
import functools

import jax
import jax.numpy as jnp
from jax import lax
from jax.experimental import pallas as pl
from jax.experimental.pallas import tpu as pltpu
from jax.sharding import PartitionSpec as P

MESH = pl.DeviceIdType.MESH
WIDE = 4096
CONTRACT_LAST = (((1,), (1,)), ((), ()))


def split_columns(start, count):
    width = min(WIDE, count)
    return [(start + step, width) for step in range(0, count, width)]


def solve(
    leaf_count,
    block_count,
    block_rows,
    live_ref,
    side_ref,
    inverse_hbm,
    update_hbm,
    forward_ref,
    backward_ref,
    inverse,
    update,
    gathered,
    pending,
    pending_in,
    reduced,
    partials,
    partials_in,
    solved,
    load_sem,
    send_sem,
    recv_sem,
):
    levels = leaf_count.bit_length()
    leaf = lax.axis_index("leaf")
    blk = lax.axis_index("blk")
    level_width = block_count * block_rows
    orders = [(1 << height) * level_width for height in range(levels)]
    sizes = [(1 << height) * block_count for height in range(levels)]
    bases = [(leaf >> height) << height for height in range(levels)]
    ranks = [(leaf - bases[height]) * block_count + blk for height in range(levels)]
    inverse_start = [((1 << height) - 1) * level_width for height in range(levels)]
    update_start = {}
    cursor = 0
    for height in range(levels):
        for ancestor in range(height + 1, levels):
            update_start[ancestor, height] = cursor
            cursor += orders[ancestor]

    loads = {}

    def load(key, hbm, vmem, start, count):
        copy = pltpu.make_async_copy(
            hbm.at[0, 0, :, pl.ds(start, count)],
            vmem.at[:, pl.ds(start, count)],
            load_sem.at[len(loads)],
        )
        copy.start()
        loads[key] = copy

    for height in range(levels):
        load(height, inverse_hbm, inverse, inverse_start[height], orders[height])
        for ancestor in range(height + 1, levels):
            key = (ancestor, height)
            load(key, update_hbm, update, update_start[key], orders[ancestor])

    barrier = pltpu.get_barrier_semaphore()
    for step in range(1, block_count):
        peer = lax.rem(blk + step, block_count)
        pl.semaphore_signal(barrier, inc=1, device_id=(leaf, peer), device_id_type=MESH)
    for step in range(1, leaf_count):
        peer = lax.rem(leaf + step, leaf_count)
        pl.semaphore_signal(barrier, inc=1, device_id=(peer, blk), device_id_type=MESH)
    pl.semaphore_wait(barrier, block_count + leaf_count - 2)

    phases = []

    def exchange(height, source, target, spread):
        size = sizes[height]
        rank = ranks[height]
        base = bases[height]
        phase = len(phases)

        def send(step, carry):
            peer = lax.rem(rank + step, size)
            pltpu.make_async_remote_copy(
                src_ref=source.at[peer] if spread else source.at[rank],
                dst_ref=target.at[rank],
                send_sem=send_sem.at[phase],
                recv_sem=recv_sem.at[phase],
                device_id=(base + peer // block_count, lax.rem(peer, block_count)),
                device_id_type=MESH,
            ).start()
            return carry

        lax.fori_loop(1, size, send, 0)
        bulk = pltpu.make_async_remote_copy(
            src_ref=target.at[pl.ds(0, size - 1)],
            dst_ref=target.at[pl.ds(0, size - 1)],
            send_sem=send_sem.at[phase],
            recv_sem=recv_sem.at[phase],
            device_id=(leaf, blk),
            device_id_type=MESH,
        )
        phases.append(bulk)
        return bulk

    def spread_rows(rows, matrix, start, count, target, add):
        for first, width in split_columns(start, count):
            product = jnp.dot(
                rows, matrix[:, first : first + width], preferred_element_type=jnp.float32
            )
            block = (first - start) // block_rows
            for step in range(width // block_rows):
                piece = product[:, step * block_rows : (step + 1) * block_rows]
                if add:
                    piece = piece + target[block + step]
                target[block + step] = piece

    def gather_rows(vector, matrix, start, count):
        total = None
        for first, width in split_columns(start, count):
            block = (first - start) // block_rows
            pieces = [vector[block + step] for step in range(width // block_rows)]
            piece = lax.dot_general(
                jnp.concatenate(pieces, axis=1).astype(jnp.bfloat16),
                matrix[:, first : first + width],
                CONTRACT_LAST,
                preferred_element_type=jnp.float32,
            )
            total = piece if total is None else total + piece
        return total

    def summed(blocks, count):
        total = blocks[0:8]
        for step in range(8, count, 8):
            total = total + blocks[step : step + 8]
        return jnp.sum(total, axis=0)

    masks = []
    for height in range(levels):
        live_count = live_ref[2 * leaf_count - (2 * leaf_count >> height) + (leaf >> height)]
        masks.append(jnp.where(ranks[height] < live_count, 1.0, 0.0).astype(jnp.float32))
    columns = [slice(height * block_rows, (height + 1) * block_rows) for height in range(levels)]

    forward = []
    for height in range(levels):
        side = side_ref[:, 0, 0, columns[height]]
        rank = ranks[height]
        if height == 0:
            vector = gathered
            vector[rank] = masks[0] * side
        else:
            incoming = pending_in[height - 1]
            vector = reduced[height - 1]
            arrival.wait_recv()
            incoming[rank] = pending[height - 1][rank]
            vector[rank] = masks[height] * (side - summed(incoming, sizes[height]))
        arrival = exchange(height, vector, vector, False)
        loads[height].wait()
        arrival.wait_recv()
        solved_rows = masks[height] * gather_rows(
            vector, inverse, inverse_start[height], orders[height]
        )
        forward.append(solved_rows)
        forward_ref[:, 0, 0, columns[height]] = solved_rows
        rows = solved_rows.astype(jnp.bfloat16)
        for ancestor in range(height + 1, levels):
            key = (ancestor, height)
            loads[key].wait()
            spread_rows(
                rows, update, update_start[key], orders[ancestor], pending[ancestor - 1], height > 0
            )
            if ancestor == height + 1:
                arrival = exchange(ancestor, pending[height], pending_in[height], True)

    residual = list(forward)
    for height in reversed(range(levels)):
        rank = ranks[height]
        rows = (masks[height] * residual[height]).astype(jnp.bfloat16)
        spread_rows(
            rows, inverse, inverse_start[height], orders[height], partials[height], False
        )
        arrival = exchange(height, partials[height], partials_in[height], True)
        if height < levels - 1:
            for lower in range(height):
                key = (height + 1, lower)
                residual[lower] = residual[lower] - gather_rows(
                    solved[height], update, update_start[key], orders[height + 1]
                )
        arrival.wait_recv()
        incoming = partials_in[height]
        incoming[rank] = partials[height][rank]
        whole = masks[height] * summed(incoming, sizes[height])
        backward_ref[:, 0, 0, columns[height]] = whole
        if height > 0:
            vector = solved[height - 1]
            vector[rank] = whole
            arrival = exchange(height, vector, vector, False)
            arrival.wait_recv()
            key = (height, height - 1)
            residual[height - 1] = residual[height - 1] - gather_rows(
                vector, update, update_start[key], orders[height]
            )

    for bulk in phases:
        bulk.wait_send()


def local(leaf_count, block_count, right_side, diag_inverse, update_factor, live_blocks):
    levels = leaf_count.bit_length()
    vectors, _, _, width = right_side.shape
    block_rows = diag_inverse.shape[2]
    sizes = [(1 << height) * block_count for height in range(levels)]

    def blocks(count):
        return pltpu.VMEM((count, vectors, block_rows), jnp.float32)

    upper = [blocks(size) for size in sizes[1:]]
    every = [blocks(size) for size in sizes]
    phases = 4 * levels - 2
    out = jax.ShapeDtypeStruct(right_side.shape, jnp.float32)
    return pl.pallas_call(
        functools.partial(solve, leaf_count, block_count, block_rows),
        out_shape=(out, out),
        in_specs=[
            pl.BlockSpec(memory_space=pltpu.SMEM),
            pl.BlockSpec(memory_space=pltpu.VMEM),
            pl.BlockSpec(memory_space=pl.ANY),
            pl.BlockSpec(memory_space=pl.ANY),
        ],
        out_specs=(
            pl.BlockSpec(memory_space=pltpu.VMEM),
            pl.BlockSpec(memory_space=pltpu.VMEM),
        ),
        scratch_shapes=[
            pltpu.VMEM(diag_inverse.shape[2:], jnp.bfloat16),
            pltpu.VMEM(update_factor.shape[2:], jnp.bfloat16),
            blocks(sizes[0]),
            upper,
            upper,
            upper,
            every,
            every,
            upper,
            pltpu.SemaphoreType.DMA((levels * (levels + 1) // 2,)),
            pltpu.SemaphoreType.DMA((phases,)),
            pltpu.SemaphoreType.DMA((phases,)),
        ],
        compiler_params=pltpu.CompilerParams(
            collective_id=0, has_side_effects=True, vmem_limit_bytes=58 << 20
        ),
        name="solve",
    )(live_blocks, right_side, diag_inverse, update_factor)


def solution(mesh):
    return jax.shard_map(
        functools.partial(local, mesh.shape["leaf"], mesh.shape["blk"]),
        mesh=mesh,
        in_specs=(
            P(None, "leaf", "blk", None),
            P("leaf", "blk", None, None),
            P("leaf", "blk", None, None),
            P(),
        ),
        out_specs=(P(None, "leaf", "blk", None), P(None, "leaf", "blk", None)),
        check_vma=False,
    )
```

time: 302 us -> 110 us (0.36)
  blocking collectives: 118 us -> 0 us
  Pallas kernels: 0 us -> 106 us
  waiting for transfers between devices: 95.2 us -> 0 us
  matrix products: 37.7 us -> 0 us
  starting transfers between devices: 27.7 us -> 0 us
  local copies, waits for them, and re-layouts: 10.9 us -> 2.59 us
  other arithmetic: 6.69 us -> 0 us
    all_to_all x10 -> x0, blocking collectives: 118 us -> none  [the longest x5 62.5 us: sent_to_all(): lax.all_to_all(jnp.broadcast_to(array[None], (count, *array.shape)), axis...]
    pallas_call x0 -> x1, Pallas kernels: none -> 106 us  [local(): pl.pallas_call(functools.partial(solve, leaf_count, block_count, block_ro...]
    all_to_all x6 -> x0, waiting for transfers between devices: 49 us -> none  [the longest x4 34 us: sent_to_all(): lax.all_to_all(jnp.broadcast_to(array[None], (count, *array.shape)), axis...]
    ppermute x12 -> x0, waiting for transfers between devices: 46.2 us -> none  [swapped(): return lax.ppermute(block, axis, route)]
    dot_general x11 -> x0, matrix products: 37.7 us -> none  [the longest x4 18.5 us: local(): jnp.dot(weighted, inverse_parts[height], preferred_element_type=jnp.float32)]
    all_to_all x6 -> x0, starting transfers between devices: 21.9 us -> none  [the longest x4 14.9 us: sent_to_all(): lax.all_to_all(jnp.broadcast_to(array[None], (count, *array.shape)), axis...]
    ppermute x12 -> x0, starting transfers between devices: 5.78 us -> none  [swapped(): return lax.ppermute(block, axis, route)]
    broadcast_in_dim x10 -> x0, local copies, waits for them, and re-layouts: 3.7 us -> none  [sent_to_all(): jnp.broadcast_to(array[None], (count, *array.shape))]
  transfers between devices with their start and end apart: 18 -> 0, of which waited for: 17 -> 0; matrix products, arithmetic and copies ran while one was open for 2% -> 0% of each run, Pallas kernels for 0% -> 0%
where the time goes in v1:
time: 110 us; the launch traced here: 109 us
  Pallas kernels  106 us (96%)
  local copies, waits for them, and re-layouts  2.59 us (2%)
    pallas_call x1, Pallas kernels, local(): pl.pallas_call(functools.partial(solve, leaf_count, block_count, block_ro...  106 us
    unnamed x2, local copies, waits for them, and re-layouts  2.59 us

profile of v1, /device:TPU:0, one launch (start us, length us, event | category | flops | bytes accessed | tf_op | source)
XLA Modules:
  0.0 109.2 jit_solution(7857069418875148882)
XLA Ops:
  0.6 105.9 %solve.1 = (f32[4,1,1,512]{3,2,1,0:T(1,128)}, f32[4,1,1,512]{3,2,1,0:T(1,128)}) custom-call(s32[15]{0:T(128)} %live_ref.1, f32[4,1,1,512]{3,2,1,0:T(1,128)} %side_ref.1, bf16[1,1,128,30720]{3,2,1,0:T(8,128)(2,1)} %inverse_hbm.1, bf16[1,1,128,69632]{3,2,1,0:T(8,128)(2,1)} %update_hbm.1), custom_call_target="tpu_custom_call" | custom-call | tf_op jit(solution)/shard_map/solve/pallas_call | solution.py:232
  106.6 1.3 %copy.8 = f32[4,1,1,512]{3,2,1,0:T(1,128)} copy(f32[4,1,1,512]{3,2,1,0:T(1,128)} %get-tuple-element.4) | data formatting | bytes 16384
  107.9 1.3 %copy.9 = f32[4,1,1,512]{3,2,1,0:T(1,128)} copy(f32[4,1,1,512]{3,2,1,0:T(1,128)} %get-tuple-element.5) | data formatting | bytes 16384

commit v2 on v1

v2 whole, which is shorter than its diff:
```python
import functools
import math

import jax
import jax.numpy as jnp
from jax import lax
from jax.experimental import pallas as pl
from jax.experimental.pallas import tpu as pltpu
from jax.sharding import PartitionSpec as P

MESH = pl.DeviceIdType.MESH
CONTRACT_LAST = (((1,), (1,)), ((), ()))


def far_first(count):
    return sorted(range(count), key=lambda step: -min(step, count - step))


def solve(
    leaf_count,
    block_count,
    block_rows,
    live_ref,
    side_ref,
    inverse_hbm,
    update_hbm,
    forward_ref,
    backward_ref,
    inverse,
    update,
    gathered,
    pending,
    pending_in,
    reduced,
    partials,
    partials_in,
    solved,
    load_sem,
    send_sem,
    recv_sem,
):
    levels = leaf_count.bit_length()
    leaf = lax.axis_index("leaf")
    blk = lax.axis_index("blk")
    level_width = block_count * block_rows
    orders = [(1 << height) * level_width for height in range(levels)]
    sizes = [(1 << height) * block_count for height in range(levels)]
    bases = [(leaf >> height) << height for height in range(levels)]
    ranks = [(leaf - bases[height]) * block_count + blk for height in range(levels)]
    inverse_start = [((1 << height) - 1) * level_width for height in range(levels)]
    update_start = {}
    cursor = 0
    for height in range(levels):
        for ancestor in range(height + 1, levels):
            update_start[ancestor, height] = cursor
            cursor += orders[ancestor]

    loads = {}

    def load(key, hbm, vmem, start, count):
        copy = pltpu.make_async_copy(
            hbm.at[0, 0, :, pl.ds(start, count)],
            vmem.at[:, pl.ds(start, count)],
            load_sem.at[len(loads)],
        )
        copy.start()
        loads[key] = copy

    for height in range(levels):
        load(height, inverse_hbm, inverse, inverse_start[height], orders[height])
        for ancestor in range(height + 1, levels):
            key = (ancestor, height)
            load(key, update_hbm, update, update_start[key], orders[ancestor])

    barrier = pltpu.get_barrier_semaphore()
    for step in range(1, block_count):
        peer = lax.rem(blk + step, block_count)
        pl.semaphore_signal(barrier, inc=1, device_id=(leaf, peer), device_id_type=MESH)
    for step in range(1, leaf_count):
        peer = lax.rem(leaf + step, leaf_count)
        pl.semaphore_signal(barrier, inc=1, device_id=(peer, blk), device_id_type=MESH)
    pl.semaphore_wait(barrier, block_count + leaf_count - 2)

    side = math.isqrt(block_count)
    row, column = blk // side, lax.rem(blk, side)
    core = lax.rem(leaf, 2)
    chips = [max(1, (1 << height) // 2) for height in range(levels)]
    cores = [min(2, 1 << height) for height in range(levels)]
    chunks = [cores[height] * block_count for height in range(levels)]
    own_chip = [(leaf - bases[height]) // 2 for height in range(levels)]
    phases = []

    def chip_at(height, step):
        return lax.rem(own_chip[height] + step, chips[height])

    def exchange(height, source, target, spread, make=None):
        phase = len(phases)
        rank = ranks[height]
        phases.append((height, target))
        for step in far_first(chips[height]):
            chip = chip_at(height, step)
            if make is not None:
                make(chip)

            def send(index, carry, step=step, chip=chip):
                away = lax.rem(side + side // 2 - index, side)
                to_row = lax.rem(row + away, side)
                for across in far_first(side):
                    to_blk = to_row * side + lax.rem(column + across, side)
                    for other in reversed(range(cores[height])):
                        if height == 0:
                            to_leaf = leaf
                        else:
                            to_leaf = bases[height] + 2 * chip + lax.rem(core + other, 2)
                        peer = (to_leaf - bases[height]) * block_count + to_blk
                        copy = pltpu.make_async_remote_copy(
                            src_ref=source.at[peer] if spread else source.at[rank],
                            dst_ref=target.at[rank],
                            send_sem=send_sem.at[phase],
                            recv_sem=recv_sem.at[phase, (chips[height] - step) % chips[height]],
                            device_id=(to_leaf, to_blk),
                            device_id_type=MESH,
                        )
                        if step == 0 and across == 0 and other == 0:
                            pl.when(away != 0)(copy.start)
                        else:
                            copy.start()
                return carry

            lax.fori_loop(0, side, send, 0)
        return phase

    def bulk(phase, count, step):
        target = phases[phase][1]
        return pltpu.make_async_remote_copy(
            src_ref=target.at[pl.ds(0, count)],
            dst_ref=target.at[pl.ds(0, count)],
            send_sem=send_sem.at[phase],
            recv_sem=recv_sem.at[phase, step],
            device_id=(leaf, blk),
            device_id_type=MESH,
        )

    def arrivals(phase):
        height = phases[phase][0]
        for step in reversed(far_first(chips[height])):
            bulk(phase, chunks[height] - (step == 0), step).wait_recv()
            yield chip_at(height, step)

    def spread_rows(height, rows, matrix, start, chip, target, add):
        count = chunks[height]
        width = count * block_rows
        first = pl.multiple_of(start + chip * width, width // cores[height])
        product = jnp.dot(
            rows, matrix[:, pl.ds(first, width)], preferred_element_type=jnp.float32
        )
        for step in range(count):
            piece = product[:, step * block_rows : (step + 1) * block_rows]
            if add:
                piece = piece + target[chip * count + step]
            target[chip * count + step] = piece

    def gather_rows(height, vector, matrix, start, chip):
        count = chunks[height]
        width = count * block_rows
        first = pl.multiple_of(start + chip * width, width // cores[height])
        pieces = [vector[chip * count + step] for step in range(count)]
        return lax.dot_general(
            jnp.concatenate(pieces, axis=1).astype(jnp.bfloat16),
            matrix[:, pl.ds(first, width)],
            CONTRACT_LAST,
            preferred_element_type=jnp.float32,
        )

    def summed(phase, source):
        height, target = phases[phase]
        target[ranks[height]] = source[ranks[height]]
        count = chunks[height]
        total = None
        for chip in arrivals(phase):
            for step in range(0, count, 8):
                piece = target[pl.ds(chip * count + step, 8)]
                total = piece if total is None else total + piece
        return jnp.sum(total, axis=0)

    masks = []
    for height in range(levels):
        live_count = live_ref[2 * leaf_count - (2 * leaf_count >> height) + (leaf >> height)]
        masks.append(jnp.where(ranks[height] < live_count, 1.0, 0.0).astype(jnp.float32))
    columns = [slice(height * block_rows, (height + 1) * block_rows) for height in range(levels)]

    forward = []
    arriving = None
    for height in range(levels):
        side_rows = side_ref[:, 0, 0, columns[height]]
        rank = ranks[height]
        if height == 0:
            vector = gathered
        else:
            vector = reduced[height - 1]
            side_rows = side_rows - summed(arriving, pending[height - 1])
        vector[rank] = masks[height] * side_rows
        phase = exchange(height, vector, vector, False)
        loads[height].wait()
        product = jnp.zeros_like(side_rows)
        for chip in arrivals(phase):
            product = product + gather_rows(
                height, vector, inverse, inverse_start[height], chip
            )
        solved_rows = masks[height] * product
        forward.append(solved_rows)
        forward_ref[:, 0, 0, columns[height]] = solved_rows
        rows = solved_rows.astype(jnp.bfloat16)
        for ancestor in range(height + 1, levels):
            key = (ancestor, height)
            loads[key].wait()

            def make(chip, ancestor=ancestor, rows=rows, key=key, add=height > 0):
                target = pending[ancestor - 1]
                spread_rows(ancestor, rows, update, update_start[key], chip, target, add)

            if ancestor == height + 1:
                arriving = exchange(
                    ancestor, pending[height], pending_in[height], True, make
                )
            else:
                for chip in range(chips[ancestor]):
                    make(chip)

    residual = list(forward)
    for height in reversed(range(levels)):
        rank = ranks[height]
        rows = (masks[height] * residual[height]).astype(jnp.bfloat16)

        def make(chip, height=height, rows=rows):
            start = inverse_start[height]
            spread_rows(height, rows, inverse, start, chip, partials[height], False)

        arriving = exchange(height, partials[height], partials_in[height], True, make)
        if height < levels - 1:
            for lower in range(height):
                for chip in range(chips[height + 1]):
                    residual[lower] = residual[lower] - gather_rows(
                        height + 1,
                        solved[height],
                        update,
                        update_start[height + 1, lower],
                        chip,
                    )
        whole = masks[height] * summed(arriving, partials[height])
        backward_ref[:, 0, 0, columns[height]] = whole
        if height > 0:
            vector = solved[height - 1]
            vector[rank] = whole
            phase = exchange(height, vector, vector, False)
            for chip in arrivals(phase):
                residual[height - 1] = residual[height - 1] - gather_rows(
                    height, vector, update, update_start[height, height - 1], chip
                )

    for phase, (height, _) in enumerate(phases):
        bulk(phase, sizes[height] - 1, 0).wait_send()


def local(leaf_count, block_count, right_side, diag_inverse, update_factor, live_blocks):
    levels = leaf_count.bit_length()
    vectors, _, _, width = right_side.shape
    block_rows = diag_inverse.shape[2]
    sizes = [(1 << height) * block_count for height in range(levels)]

    def blocks(count):
        return pltpu.VMEM((count, vectors, block_rows), jnp.float32)

    upper = [blocks(size) for size in sizes[1:]]
    every = [blocks(size) for size in sizes]
    phases = 4 * levels - 2
    out = jax.ShapeDtypeStruct(right_side.shape, jnp.float32)
    return pl.pallas_call(
        functools.partial(solve, leaf_count, block_count, block_rows),
        out_shape=(out, out),
        in_specs=[
            pl.BlockSpec(memory_space=pltpu.SMEM),
            pl.BlockSpec(memory_space=pltpu.VMEM),
            pl.BlockSpec(memory_space=pl.ANY),
            pl.BlockSpec(memory_space=pl.ANY),
        ],
        out_specs=(
            pl.BlockSpec(memory_space=pltpu.VMEM),
            pl.BlockSpec(memory_space=pltpu.VMEM),
        ),
        scratch_shapes=[
            pltpu.VMEM(diag_inverse.shape[2:], jnp.bfloat16),
            pltpu.VMEM(update_factor.shape[2:], jnp.bfloat16),
            blocks(sizes[0]),
            upper,
            upper,
            upper,
            every,
            every,
            upper,
            pltpu.SemaphoreType.DMA((levels * (levels + 1) // 2,)),
            pltpu.SemaphoreType.DMA((phases,)),
            pltpu.SemaphoreType.DMA((phases, max(1, leaf_count // 2))),
        ],
        compiler_params=pltpu.CompilerParams(
            collective_id=0, has_side_effects=True, vmem_limit_bytes=58 << 20
        ),
        name="solve",
    )(live_blocks, right_side, diag_inverse, update_factor)


def solution(mesh):
    return jax.shard_map(
        functools.partial(local, mesh.shape["leaf"], mesh.shape["blk"]),
        mesh=mesh,
        in_specs=(
            P(None, "leaf", "blk", None),
            P("leaf", "blk", None, None),
            P("leaf", "blk", None, None),
            P(),
        ),
        out_specs=(P(None, "leaf", "blk", None), P(None, "leaf", "blk", None)),
        check_vma=False,
    )
```

time: 110 us -> 102 us (0.927)
  Pallas kernels: 106 us -> 98.5 us
    pallas_call x1, Pallas kernels: 106 us -> 98.5 us  [local(): pl.pallas_call(functools.partial(solve, leaf_count, block_count, block_ro...]
where the time goes in v2:
time: 102 us
  Pallas kernels  98.5 us (97%)
  local copies, waits for them, and re-layouts  2.59 us (3%)
    pallas_call x1, Pallas kernels, local(): pl.pallas_call(functools.partial(solve, leaf_count, block_count, block_ro...  98.5 us
    unnamed x2, local copies, waits for them, and re-layouts  2.59 us

profile of v2, /device:TPU:0, one launch (start us, length us, event | category | flops | bytes accessed | tf_op | source)
XLA Modules:
  0.0 101.8 jit_solution(15334388490468409598)
XLA Ops:
  0.6 98.5 %solve.1 = (f32[4,1,1,512]{3,2,1,0:T(1,128)}, f32[4,1,1,512]{3,2,1,0:T(1,128)}) custom-call(s32[15]{0:T(128)} %live_ref.1, f32[4,1,1,512]{3,2,1,0:T(1,128)} %side_ref.1, bf16[1,1,128,30720]{3,2,1,0:T(8,128)(2,1)} %inverse_hbm.1, bf16[1,1,128,69632]{3,2,1,0:T(8,128)(2,1)} %update_hbm.1), custom_call_target="tpu_custom_call" | custom-call | tf_op jit(solution)/shard_map/solve/pallas_call | solution.py:278
  99.2 1.3 %copy.8 = f32[4,1,1,512]{3,2,1,0:T(1,128)} copy(f32[4,1,1,512]{3,2,1,0:T(1,128)} %get-tuple-element.4) | data formatting | bytes 16384
  100.5 1.3 %copy.9 = f32[4,1,1,512]{3,2,1,0:T(1,128)} copy(f32[4,1,1,512]{3,2,1,0:T(1,128)} %get-tuple-element.5) | data formatting | bytes 16384

commit v3 on v2

v3 whole, which is shorter than its diff:
```python
import functools
import itertools
import math

import jax
import jax.numpy as jnp
from jax import lax
from jax.experimental import pallas as pl
from jax.experimental.pallas import tpu as pltpu
from jax.sharding import PartitionSpec as P

MESH = pl.DeviceIdType.MESH
EARLY = 2
PLACE = pltpu.VMEM
USE_WIDE = False
CONTRACT_LAST = (((1,), (1,)), ((), ()))


def ring(step, count):
    return min(step, count - step)


def solve(
    leaf_count,
    block_count,
    block_rows,
    live_ref,
    side_ref,
    inverse_hbm,
    update_hbm,
    forward_ref,
    backward_ref,
    inverse,
    update,
    gathered,
    pending,
    pending_in,
    reduced,
    partials,
    partials_in,
    solved,
    load_sem,
    send_sem,
    recv_sem,
):
    levels = leaf_count.bit_length()
    leaf = lax.axis_index("leaf")
    blk = lax.axis_index("blk")
    level_width = block_count * block_rows
    orders = [(1 << height) * level_width for height in range(levels)]
    sizes = [(1 << height) * block_count for height in range(levels)]
    bases = [(leaf >> height) << height for height in range(levels)]
    ranks = [(leaf - bases[height]) * block_count + blk for height in range(levels)]
    inverse_start = [((1 << height) - 1) * level_width for height in range(levels)]
    update_start = {}
    cursor = 0
    for height in range(levels):
        for ancestor in range(height + 1, levels):
            update_start[ancestor, height] = cursor
            cursor += orders[ancestor]

    loads = {}

    def load(key, hbm, vmem, start, count):
        copy = pltpu.make_async_copy(
            hbm.at[0, 0, :, pl.ds(start, count)],
            vmem.at[:, pl.ds(start, count)],
            load_sem.at[len(loads)],
        )
        copy.start()
        loads[key] = copy

    for height in range(levels):
        load(height, inverse_hbm, inverse, inverse_start[height], orders[height])
        for ancestor in range(height + 1, levels):
            key = (ancestor, height)
            load(key, update_hbm, update, update_start[key], orders[ancestor])

    barrier = pltpu.get_barrier_semaphore()
    for step in range(1, block_count):
        peer = lax.rem(blk + step, block_count)
        pl.semaphore_signal(barrier, inc=1, device_id=(leaf, peer), device_id_type=MESH)
    for step in range(1, leaf_count):
        peer = lax.rem(leaf + step, leaf_count)
        pl.semaphore_signal(barrier, inc=1, device_id=(peer, blk), device_id_type=MESH)
    pl.semaphore_wait(barrier, block_count + leaf_count - 2)

    side = math.isqrt(block_count)
    core = lax.rem(leaf, 2)
    chips = [max(1, (1 << height) // 2) for height in range(levels)]
    cores = [min(2, 1 << height) for height in range(levels)]
    to_row = [lax.rem(blk // side + step, side) for step in range(side)]
    to_column = [lax.rem(blk + step, side) for step in range(side)]
    to_blk = {
        (down, across): to_row[down] * side + to_column[across]
        for down in range(side)
        for across in range(side)
    }
    to_leaf = {(0, 0, 0): 0}
    for height in range(1, levels):
        own_chip = (leaf - bases[height]) // 2
        for step in range(chips[height]):
            chip = lax.rem(own_chip + step, chips[height])
            for other in range(2):
                to_leaf[height, step, other] = 2 * chip + lax.rem(core + other, 2)
    phases = []

    def hops(height, step, down, across):
        return ring(step, chips[height]) + ring(down, side) + ring(across, side)

    def exchange(height, source, target, make=None):
        phase = len(phases)
        rank = ranks[height]
        phases.append((height, target))
        paths = sorted(
            itertools.product(
                range(chips[height]), range(side), range(side), reversed(range(cores[height]))
            ),
            key=lambda path: -hops(height, *path[:3]),
        )
        longest = hops(height, *paths[0][:3])

        def send(step, down, across, other):
            if step == down == across == other == 0:
                return
            place = to_leaf[height, step, other]
            peer = place * block_count + to_blk[down, across]
            arrival = (chips[height] - step) % chips[height] * 2 + other
            pltpu.make_async_remote_copy(
                src_ref=source.at[rank if make is None else peer],
                dst_ref=target.at[rank],
                send_sem=send_sem.at[phase],
                recv_sem=recv_sem.at[phase, arrival],
                device_id=(bases[height] + place, to_blk[down, across]),
                device_id_type=MESH,
            ).start()

        held = []
        for step in sorted(range(chips[height]), key=lambda step: -ring(step, chips[height])):
            if make is not None:
                make(step)
            for path in paths:
                if path[0] != step:
                    continue
                if make is not None and hops(height, *path[:3]) >= longest - EARLY:
                    send(*path)
                else:
                    held.append(path)
        for path in sorted(held, key=paths.index):
            send(*path)
        return phase

    def bulk(phase, count, arrival):
        target = phases[phase][1]
        return pltpu.make_async_remote_copy(
            src_ref=target.at[pl.ds(0, count)],
            dst_ref=target.at[pl.ds(0, count)],
            send_sem=send_sem.at[phase],
            recv_sem=recv_sem.at[phase, arrival],
            device_id=(leaf, blk),
            device_id_type=MESH,
        )

    def arrivals(phase):
        height = phases[phase][0]
        for step in sorted(range(chips[height]), key=lambda step: ring(step, chips[height])):
            leaves = []
            for other in range(cores[height]):
                count = block_count - (step == other == 0)
                bulk(phase, count, step * 2 + other).wait_recv()
                leaves.append(to_leaf[height, step, other])
                if not USE_WIDE:
                    yield leaves[0], 1
                    leaves = []
            if leaves:
                yield leaves[0] // 2 * 2 if height > 0 else 0, len(leaves)

    def spread_rows(rows, matrix, start, first, count, target, add):
        column = pl.multiple_of(start + first * level_width, level_width)
        product = jnp.dot(
            rows, matrix[:, pl.ds(column, count * level_width)], preferred_element_type=jnp.float32
        )
        for step in range(count * block_count):
            piece = product[:, step * block_rows : (step + 1) * block_rows]
            if add:
                piece = piece + target[first * block_count + step]
            target[first * block_count + step] = piece

    def gather_rows(vector, matrix, start, first, count):
        column = pl.multiple_of(start + first * level_width, level_width)
        pieces = [vector[first * block_count + step] for step in range(count * block_count)]
        return lax.dot_general(
            jnp.concatenate(pieces, axis=1).astype(jnp.bfloat16),
            matrix[:, pl.ds(column, count * level_width)],
            CONTRACT_LAST,
            preferred_element_type=jnp.float32,
        )

    def summed(phase, source):
        height, target = phases[phase]
        target[ranks[height]] = source[ranks[height]]
        total = None
        for first, count in arrivals(phase):
            for step in range(0, count * block_count, 8):
                piece = target[pl.ds(first * block_count + step, 8)]
                total = piece if total is None else total + piece
        return jnp.sum(total, axis=0)

    masks = []
    for height in range(levels):
        live_count = live_ref[2 * leaf_count - (2 * leaf_count >> height) + (leaf >> height)]
        masks.append(jnp.where(ranks[height] < live_count, 1.0, 0.0).astype(jnp.float32))
    columns = [slice(height * block_rows, (height + 1) * block_rows) for height in range(levels)]

    forward = []
    arriving = None
    for height in range(levels):
        side_rows = side_ref[:, 0, 0, columns[height]]
        rank = ranks[height]
        if height == 0:
            vector = gathered
        else:
            vector = reduced[height - 1]
            side_rows = side_rows - summed(arriving, pending[height - 1])
        vector[rank] = masks[height] * side_rows
        phase = exchange(height, vector, vector)
        loads[height].wait()
        product = jnp.zeros_like(side_rows)
        for first, count in arrivals(phase):
            product = product + gather_rows(
                    vector, inverse, inverse_start[height], first, count
                )
        solved_rows = masks[height] * product
        forward.append(solved_rows)
        forward_ref[:, 0, 0, columns[height]] = solved_rows
        rows = solved_rows.astype(jnp.bfloat16)
        for ancestor in range(height + 1, levels):
            key = (ancestor, height)
            loads[key].wait()

            def spread(first, ancestor=ancestor, rows=rows, key=key, add=height > 0):
                target = pending[ancestor - 1]
                spread_rows(rows, update, update_start[key], first, 2, target, add)

            if ancestor == height + 1:

                def make(step, ancestor=ancestor, spread=spread):
                    spread(to_leaf[ancestor, step, 0] // 2 * 2)

                arriving = exchange(ancestor, pending[height], pending_in[height], make)
            else:
                for first in range(0, 1 << ancestor, 2):
                    spread(first)

    residual = list(forward)
    for height in reversed(range(levels)):
        rank = ranks[height]
        rows = (masks[height] * residual[height]).astype(jnp.bfloat16)

        def make(step, height=height, rows=rows):
            first = to_leaf[height, step, 0] // 2 * 2
            spread_rows(
                rows,
                inverse,
                inverse_start[height],
                first,
                cores[height],
                partials[height],
                False,
            )

        arriving = exchange(height, partials[height], partials_in[height], make)
        if height < levels - 1:
            for lower in range(height):
                start = update_start[height + 1, lower]
                for first in range(0, 2 << height, 2):
                    residual[lower] = residual[lower] - gather_rows(
                        solved[height], update, start, first, 2
                    )
        whole = masks[height] * summed(arriving, partials[height])
        backward_ref[:, 0, 0, columns[height]] = whole
        if height > 0:
            vector = solved[height - 1]
            vector[rank] = whole
            phase = exchange(height, vector, vector)
            for first, count in arrivals(phase):
                residual[height - 1] = residual[height - 1] - gather_rows(
                    vector, update, update_start[height, height - 1], first, count
                )

    for phase, (height, _) in enumerate(phases):
        bulk(phase, sizes[height] - 1, 0).wait_send()


def place(forward_ref, backward_ref, forward_out, backward_out, sem):
    first = pltpu.make_async_copy(forward_ref, forward_out, sem.at[0])
    second = pltpu.make_async_copy(backward_ref, backward_out, sem.at[1])
    first.start()
    second.start()
    first.wait()
    second.wait()


def local(leaf_count, block_count, right_side, diag_inverse, update_factor, live_blocks):
    levels = leaf_count.bit_length()
    vectors, _, _, width = right_side.shape
    block_rows = diag_inverse.shape[2]
    sizes = [(1 << height) * block_count for height in range(levels)]

    def blocks(count):
        return pltpu.VMEM((count, vectors, block_rows), jnp.float32)

    upper = [blocks(size) for size in sizes[1:]]
    every = [blocks(size) for size in sizes]
    phases = 4 * levels - 2
    out = jax.ShapeDtypeStruct(right_side.shape, jnp.float32)
    solutions = pl.pallas_call(
        functools.partial(solve, leaf_count, block_count, block_rows),
        out_shape=(out, out),
        in_specs=[
            pl.BlockSpec(memory_space=pltpu.SMEM),
            pl.BlockSpec(memory_space=pltpu.VMEM),
            pl.BlockSpec(memory_space=pl.ANY),
            pl.BlockSpec(memory_space=pl.ANY),
        ],
        out_specs=(
            pl.BlockSpec(memory_space=pltpu.VMEM),
            pl.BlockSpec(memory_space=pltpu.VMEM),
        ),
        scratch_shapes=[
            pltpu.VMEM(diag_inverse.shape[2:], jnp.bfloat16),
            pltpu.VMEM(update_factor.shape[2:], jnp.bfloat16),
            blocks(sizes[0]),
            upper,
            upper,
            upper,
            every,
            every,
            upper,
            pltpu.SemaphoreType.DMA((levels * (levels + 1) // 2,)),
            pltpu.SemaphoreType.DMA((phases,)),
            pltpu.SemaphoreType.DMA((phases, leaf_count)),
        ],
        compiler_params=pltpu.CompilerParams(
            collective_id=0, has_side_effects=True, vmem_limit_bytes=58 << 20
        ),
        name="solve",
    )(live_blocks, right_side, diag_inverse, update_factor)
    return pl.pallas_call(
        place,
        out_shape=(out, out),
        in_specs=[pl.BlockSpec(memory_space=PLACE)] * 2,
        out_specs=(pl.BlockSpec(memory_space=pl.ANY),) * 2,
        scratch_shapes=[pltpu.SemaphoreType.DMA((2,))],
        name="place",
    )(*solutions)


def solution(mesh):
    return jax.shard_map(
        functools.partial(local, mesh.shape["leaf"], mesh.shape["blk"]),
        mesh=mesh,
        in_specs=(
            P(None, "leaf", "blk", None),
            P("leaf", "blk", None, None),
            P("leaf", "blk", None, None),
            P(),
        ),
        out_specs=(P(None, "leaf", "blk", None), P(None, "leaf", "blk", None)),
        check_vma=False,
    )
```

time: 102 us -> 99 us (0.971)
  local copies, waits for them, and re-layouts: 2.59 us -> 0 us
    unnamed x2 -> x0, local copies, waits for them, and re-layouts: 2.59 us -> none
    pallas_call x1, Pallas kernels: 98.5 us -> 96.6 us  [local(): pl.pallas_call(functools.partial(solve, leaf_count, block_count, block_ro...]
    pallas_call x0 -> x1, Pallas kernels: none -> 1.33 us  [local(): pl.pallas_call(place, out_shape=(out, out), in_specs=[pl.BlockSpec(memory...]
where the time goes in v3:
time: 99 us; the launch traced here: 98.7 us
  Pallas kernels  97.9 us (99%)
    pallas_call x1, Pallas kernels, local(): pl.pallas_call(functools.partial(solve, leaf_count, block_count, block_ro...  96.6 us

profile of v3, /device:TPU:0, one launch (start us, length us, event | category | flops | bytes accessed | tf_op | source)
XLA Modules:
  0.0 98.7 jit_solution(14020171756039324456)
XLA Ops:
  0.6 96.6 %solve.1 = (f32[4,1,1,512]{3,2,1,0:T(1,128)}, f32[4,1,1,512]{3,2,1,0:T(1,128)}) custom-call(s32[15]{0:T(128)} %live_ref.1, f32[4,1,1,512]{3,2,1,0:T(1,128)} %side_ref.1, bf16[1,1,128,30720]{3,2,1,0:T(8,128)(2,1)} %inverse_hbm.1, bf16[1,1,128,69632]{3,2,1,0:T(8,128)(2,1)} %update_hbm.1), custom_call_target="tpu_custom_call" | custom-call | tf_op jit(solution)/shard_map/solve/pallas_call | solution.py:317
  97.3 1.3 %place.1 = (f32[4,1,1,512]{3,2,1,0:T(1,128)}, f32[4,1,1,512]{3,2,1,0:T(1,128)}) custom-call(f32[4,1,1,512]{3,2,1,0:T(1,128)} %get-tuple-element.4.forward_ref, f32[4,1,1,512]{3,2,1,0:T(1,128)} %get-tuple-element.5.backward_ref), custom_call_target="tpu_custom_call" | custom-call | tf_op jit(solution)/shard_map/place/pallas_call | solution.py:349

commit v4 on v3

--- a/solution.py
+++ b/solution.py
@@ -39,6 +39,8 @@
     partials,
     partials_in,
     solved,
+    one_row,
+    eight_rows,
     load_sem,
     send_sem,
     recv_sem,
@@ -103,15 +105,29 @@
             chip = lax.rem(own_chip + step, chips[height])
             for other in range(2):
                 to_leaf[height, step, other] = 2 * chip + lax.rem(core + other, 2)
+    own_chips = [(leaf - bases[height]) // 2 for height in range(levels)]
     phases = []
+
+    def guarded(condition, body):
+        if condition is None:
+            body()
+        else:
+            pl.when(condition)(body)
+
+    def meets(height, step, upward):
+        if upward is None or step == 0:
+            return None
+        if upward:
+            return own_chips[height] + step < chips[height]
+        return own_chips[height] + step >= chips[height]
 
     def hops(height, step, down, across):
         return ring(step, chips[height]) + ring(down, side) + ring(across, side)
 
-    def exchange(height, source, target, make=None):
+    def exchange(height, source, target, make=None, upward=None):
         phase = len(phases)
         rank = ranks[height]
-        phases.append((height, target))
+        phases.append((height, target, upward))
         paths = sorted(
             itertools.product(
                 range(chips[height]), range(side), range(side), reversed(range(cores[height]))
@@ -137,15 +153,19 @@
 
         held = []
         for step in sorted(range(chips[height]), key=lambda step: -ring(step, chips[height])):
-            if make is not None:
-                make(step)
-            for path in paths:
-                if path[0] != step:
-                    continue
-                if make is not None and hops(height, *path[:3]) >= longest - EARLY:
-                    send(*path)
-                else:
-                    held.append(path)
+            reach = [path for path in paths if path[0] == step]
+
+            def serve(step=step, reach=reach):
+                if make is not None:
+                    make(step)
+                for path in reach:
+                    late = hops(height, *path[:3]) < longest - EARLY
+                    if upward is None and (make is None or late):
+                        held.append(path)
+                    else:
+                        send(*path)
+
+            guarded(meets(height, step, upward), serve)
         for path in sorted(held, key=paths.index):
             send(*path)
         return phase
@@ -161,19 +181,37 @@
             device_id_type=MESH,
         )
 
-    def arrivals(phase):
-        height = phases[phase][0]
+    def receive(phase, use):
+        height, _, upward = phases[phase]
         for step in sorted(range(chips[height]), key=lambda step: ring(step, chips[height])):
-            leaves = []
-            for other in range(cores[height]):
-                count = block_count - (step == other == 0)
-                bulk(phase, count, step * 2 + other).wait_recv()
-                leaves.append(to_leaf[height, step, other])
-                if not USE_WIDE:
-                    yield leaves[0], 1
-                    leaves = []
-            if leaves:
-                yield leaves[0] // 2 * 2 if height > 0 else 0, len(leaves)
+
+            def take(step=step):
+                for other in range(cores[height]):
+                    count = block_count - (step == other == 0)
+                    bulk(phase, count, step * 2 + other).wait_recv()
+                    if not USE_WIDE:
+                        use(to_leaf[height, step, other], 1)
+                if USE_WIDE:
+                    use(to_leaf[height, step, 0] // 2 * 2 if height > 0 else 0, cores[height])
+
+            guarded(meets(height, step, None if upward is None else not upward), take)
+
+    def collect(phase, term, held):
+        if phases[phase][2] is None:
+            terms = []
+            receive(phase, lambda first, count: terms.append(term(first, count)))
+            return functools.reduce(jnp.add, terms)
+        fresh = [True]
+
+        def use(first, count):
+            if fresh[0]:
+                held[...] = term(first, count)
+                fresh[0] = False
+            else:
+                held[...] = held[...] + term(first, count)
+
+        receive(phase, use)
+        return held[...]
 
     def spread_rows(rows, matrix, start, first, count, target, add):
         column = pl.multiple_of(start + first * level_width, level_width)
@@ -197,14 +235,17 @@
         )
 
     def summed(phase, source):
-        height, target = phases[phase]
+        height, target, _ = phases[phase]
         target[ranks[height]] = source[ranks[height]]
-        total = None
-        for first, count in arrivals(phase):
+
+        def term(first, count):
+            total = None
             for step in range(0, count * block_count, 8):
                 piece = target[pl.ds(first * block_count + step, 8)]
                 total = piece if total is None else total + piece
-        return jnp.sum(total, axis=0)
+            return total
+
+        return jnp.sum(collect(phase, term, eight_rows), axis=0)
 
     masks = []
     for height in range(levels):
@@ -223,13 +264,14 @@
             vector = reduced[height - 1]
             side_rows = side_rows - summed(arriving, pending[height - 1])
         vector[rank] = masks[height] * side_rows
-        phase = exchange(height, vector, vector)
+        phase = exchange(height, vector, vector, upward=True if chips[height] > 1 else None)
         loads[height].wait()
-        product = jnp.zeros_like(side_rows)
-        for first, count in arrivals(phase):
-            product = product + gather_rows(
-                    vector, inverse, inverse_start[height], first, count
-                )
+        start = inverse_start[height]
+        product = collect(
+            phase,
+            lambda first, count: gather_rows(vector, inverse, start, first, count),
+            one_row,
+        )
         solved_rows = masks[height] * product
         forward.append(solved_rows)
         forward_ref[:, 0, 0, columns[height]] = solved_rows
@@ -269,7 +311,8 @@
                 False,
             )
 
-        arriving = exchange(height, partials[height], partials_in[height], make)
+        upward = False if chips[height] > 1 else None
+        arriving = exchange(height, partials[height], partials_in[height], make, upward)
         if height < levels - 1:
             for lower in range(height):
                 start = update_start[height + 1, lower]
@@ -283,13 +326,20 @@
             vector = solved[height - 1]
             vector[rank] = whole
             phase = exchange(height, vector, vector)
-            for first, count in arrivals(phase):
-                residual[height - 1] = residual[height - 1] - gather_rows(
-                    vector, update, update_start[height, height - 1], first, count
-                )
-
-    for phase, (height, _) in enumerate(phases):
-        bulk(phase, sizes[height] - 1, 0).wait_send()
+            start = update_start[height, height - 1]
+            residual[height - 1] = residual[height - 1] - collect(
+                phase,
+                lambda first, count: gather_rows(vector, update, start, first, count),
+                one_row,
+            )
+
+    for phase, (height, _, upward) in enumerate(phases):
+        if upward is None:
+            bulk(phase, sizes[height] - 1, 0).wait_send()
+            continue
+        for step in range(chips[height]):
+            count = cores[height] * block_count - (step == 0)
+            guarded(meets(height, step, upward), bulk(phase, count, 0).wait_send)
 
 
 def place(forward_ref, backward_ref, forward_out, backward_out, sem):
@@ -337,6 +387,8 @@
             every,
             every,
             upper,
+            pltpu.VMEM((vectors, block_rows), jnp.float32),
+            blocks(8),
             pltpu.SemaphoreType.DMA((levels * (levels + 1) // 2,)),
             pltpu.SemaphoreType.DMA((phases,)),
             pltpu.SemaphoreType.DMA((phases, leaf_count)),

time: 99 us -> 96.3 us (0.973)
  Pallas kernels: 97.9 us -> 95.3 us
    pallas_call x1, Pallas kernels: 96.6 us -> 94 us  [local(): pl.pallas_call(functools.partial(solve, leaf_count, block_count, block_ro...]
where the time goes in v4:
time: 96.3 us; the launch traced here: 96.1 us
  Pallas kernels  95.3 us (99%)
    pallas_call x1, Pallas kernels, local(): pl.pallas_call(functools.partial(solve, leaf_count, block_count, block_ro...  94 us

profile of v4, /device:TPU:0, one launch (start us, length us, event | category | flops | bytes accessed | tf_op | source)
XLA Modules:
  0.0 96.1 jit_solution(15440902802738111865)
XLA Ops:
  0.6 94.0 %solve.1 = (f32[4,1,1,512]{3,2,1,0:T(1,128)}, f32[4,1,1,512]{3,2,1,0:T(1,128)}) custom-call(s32[15]{0:T(128)} %live_ref.1, f32[4,1,1,512]{3,2,1,0:T(1,128)} %side_ref.1, bf16[1,1,128,30720]{3,2,1,0:T(8,128)(2,1)} %inverse_hbm.1, bf16[1,1,128,69632]{3,2,1,0:T(8,128)(2,1)} %update_hbm.1), custom_call_target="tpu_custom_call" | custom-call | tf_op jit(solution)/shard_map/solve/pallas_call | solution.py:367
  94.6 1.3 %place.1 = (f32[4,1,1,512]{3,2,1,0:T(1,128)}, f32[4,1,1,512]{3,2,1,0:T(1,128)}) custom-call(f32[4,1,1,512]{3,2,1,0:T(1,128)} %get-tuple-element.4.forward_ref, f32[4,1,1,512]{3,2,1,0:T(1,128)} %get-tuple-element.5.backward_ref), custom_call_target="tpu_custom_call" | custom-call | tf_op jit(solution)/shard_map/place/pallas_call | solution.py:401

commit v5 on v4

--- a/solution.py
+++ b/solution.py
@@ -11,8 +11,6 @@
 
 MESH = pl.DeviceIdType.MESH
 EARLY = 2
-PLACE = pltpu.VMEM
-USE_WIDE = False
 CONTRACT_LAST = (((1,), (1,)), ((), ()))
 
 
@@ -114,9 +112,11 @@
         else:
             pl.when(condition)(body)
 
-    def meets(height, step, upward):
-        if upward is None or step == 0:
+    def meets(height, step, other, upward):
+        if upward is None or step == other == 0:
             return None
+        if step == 0:
+            return core == (0 if upward else 1)
         if upward:
             return own_chips[height] + step < chips[height]
         return own_chips[height] + step >= chips[height]
@@ -160,12 +160,23 @@
                     make(step)
                 for path in reach:
                     late = hops(height, *path[:3]) < longest - EARLY
+                    if upward is not None and step == 0:
+                        continue
                     if upward is None and (make is None or late):
                         held.append(path)
                     else:
                         send(*path)
 
-            guarded(meets(height, step, upward), serve)
+            guarded(None if step == 0 else meets(height, step, 0, upward), serve)
+            if upward is not None and step == 0:
+                for other in reversed(range(cores[height])):
+
+                    def share(other=other, reach=reach):
+                        for path in reach:
+                            if path[3] == other:
+                                send(*path)
+
+                    guarded(meets(height, 0, other, upward), share)
         for path in sorted(held, key=paths.index):
             send(*path)
         return phase
@@ -185,16 +196,15 @@
         height, _, upward = phases[phase]
         for step in sorted(range(chips[height]), key=lambda step: ring(step, chips[height])):
 
-            def take(step=step):
-                for other in range(cores[height]):
+            for other in range(cores[height]):
+
+                def take(step=step, other=other):
                     count = block_count - (step == other == 0)
                     bulk(phase, count, step * 2 + other).wait_recv()
-                    if not USE_WIDE:
-                        use(to_leaf[height, step, other], 1)
-                if USE_WIDE:
-                    use(to_leaf[height, step, 0] // 2 * 2 if height > 0 else 0, cores[height])
-
-            guarded(meets(height, step, None if upward is None else not upward), take)
+                    use(to_leaf[height, step, other], 1)
+
+                needed = None if upward is None else not upward
+                guarded(meets(height, step, other, needed), take)
 
     def collect(phase, term, held):
         if phases[phase][2] is None:
@@ -264,7 +274,7 @@
             vector = reduced[height - 1]
             side_rows = side_rows - summed(arriving, pending[height - 1])
         vector[rank] = masks[height] * side_rows
-        phase = exchange(height, vector, vector, upward=True if chips[height] > 1 else None)
+        phase = exchange(height, vector, vector, upward=True if height > 0 else None)
         loads[height].wait()
         start = inverse_start[height]
         product = collect(
@@ -311,7 +321,7 @@
                 False,
             )
 
-        upward = False if chips[height] > 1 else None
+        upward = False if height > 0 else None
         arriving = exchange(height, partials[height], partials_in[height], make, upward)
         if height < levels - 1:
             for lower in range(height):
@@ -337,9 +347,9 @@
         if upward is None:
             bulk(phase, sizes[height] - 1, 0).wait_send()
             continue
-        for step in range(chips[height]):
-            count = cores[height] * block_count - (step == 0)
-            guarded(meets(height, step, upward), bulk(phase, count, 0).wait_send)
+        for step, other in itertools.product(range(chips[height]), range(cores[height])):
+            count = block_count - (step == other == 0)
+            guarded(meets(height, step, other, upward), bulk(phase, count, 0).wait_send)
 
 
 def place(forward_ref, backward_ref, forward_out, backward_out, sem):
@@ -364,9 +374,10 @@
     every = [blocks(size) for size in sizes]
     phases = 4 * levels - 2
     out = jax.ShapeDtypeStruct(right_side.shape, jnp.float32)
+    kept = pltpu.VMEM(right_side.shape, jnp.float32)
     solutions = pl.pallas_call(
         functools.partial(solve, leaf_count, block_count, block_rows),
-        out_shape=(out, out),
+        out_shape=(kept, kept),
         in_specs=[
             pl.BlockSpec(memory_space=pltpu.SMEM),
             pl.BlockSpec(memory_space=pltpu.VMEM),
@@ -401,7 +412,8 @@
     return pl.pallas_call(
         place,
         out_shape=(out, out),
-        in_specs=[pl.BlockSpec(memory_space=PLACE)] * 2,
+        in_specs=[pl.BlockSpec(memory_space=pltpu.VMEM)] * 2,
+        compiler_params=pltpu.CompilerParams(vmem_limit_bytes=1 << 20),
         out_specs=(pl.BlockSpec(memory_space=pl.ANY),) * 2,
         scratch_shapes=[pltpu.SemaphoreType.DMA((2,))],
         name="place",

time: 96.3 us -> 93.8 us (0.974)
  Pallas kernels: 95.3 us -> 92.8 us
    pallas_call x1, Pallas kernels: 94 us -> 92.2 us  [local(): pl.pallas_call(functools.partial(solve, leaf_count, block_count, block_ro...]
where the time goes in v5:
time: 93.8 us; the launch traced here: 93.6 us
  Pallas kernels  92.8 us (99%)
    pallas_call x1, Pallas kernels, local(): pl.pallas_call(functools.partial(solve, leaf_count, block_count, block_ro...  92.2 us

profile of v5, /device:TPU:0, one launch (start us, length us, event | category | flops | bytes accessed | tf_op | source)
XLA Modules:
  0.0 93.6 jit_solution(824408961951078444)
XLA Ops:
  0.6 92.2 %solve.1 = (f32[4,1,1,512]{3,2,1,0:T(1,128)S(1)}, f32[4,1,1,512]{3,2,1,0:T(1,128)S(1)}) custom-call(s32[15]{0:T(128)} %live_ref.1, f32[4,1,1,512]{3,2,1,0:T(1,128)} %side_ref.1, bf16[1,1,128,30720]{3,2,1,0:T(8,128)(2,1)} %inverse_hbm.1, bf16[1,1,128,69632]{3,2,1,0:T(8,128)(2,1)} %update_hbm.1), custom_call_target="tpu_custom_call" | custom-call | tf_op jit(solution)/shard_map/solve/pallas_call | solution.py:378
  92.8 0.6 place.1

commit v6 on v5

--- a/solution.py
+++ b/solution.py
@@ -77,10 +77,16 @@
             load(key, update_hbm, update, update_start[key], orders[ancestor])
 
     barrier = pltpu.get_barrier_semaphore()
-    for step in range(1, block_count):
-        peer = lax.rem(blk + step, block_count)
+    edge = math.isqrt(block_count)
+    for down, across in sorted(
+        itertools.product(range(edge), range(edge)),
+        key=lambda way: -ring(way[0], edge) - ring(way[1], edge),
+    ):
+        if down == across == 0:
+            continue
+        peer = lax.rem(blk // edge + down, edge) * edge + lax.rem(blk + across, edge)
         pl.semaphore_signal(barrier, inc=1, device_id=(leaf, peer), device_id_type=MESH)
-    for step in range(1, leaf_count):
+    for step in sorted(range(1, leaf_count), key=lambda step: -ring(step, leaf_count)):
         peer = lax.rem(leaf + step, leaf_count)
         pl.semaphore_signal(barrier, inc=1, device_id=(peer, blk), device_id_type=MESH)
     pl.semaphore_wait(barrier, block_count + leaf_count - 2)

time: 93.8 us -> 93.8 us (level)
  no operation moved by 1% of the time
where the time goes in v6:
time: 93.8 us; the launch traced here: 93.6 us
  Pallas kernels  92.8 us (99%)
    pallas_call x1, Pallas kernels, local(): pl.pallas_call(functools.partial(solve, leaf_count, block_count, block_ro...  92.2 us

profile of v6, /device:TPU:0, one launch (start us, length us, event | category | flops | bytes accessed | tf_op | source)
XLA Modules:
  0.0 93.6 jit_solution(3683933739473085999)
XLA Ops:
  0.6 92.2 %solve.1 = (f32[4,1,1,512]{3,2,1,0:T(1,128)S(1)}, f32[4,1,1,512]{3,2,1,0:T(1,128)S(1)}) custom-call(s32[15]{0:T(128)} %live_ref.1, f32[4,1,1,512]{3,2,1,0:T(1,128)} %side_ref.1, bf16[1,1,128,30720]{3,2,1,0:T(8,128)(2,1)} %inverse_hbm.1, bf16[1,1,128,69632]{3,2,1,0:T(8,128)(2,1)} %update_hbm.1), custom_call_target="tpu_custom_call" | custom-call | tf_op jit(solution)/shard_map/solve/pallas_call | solution.py:384
  92.8 0.6 place.1
